TPU v7x, 32 devices: a whole 2x2x4 slice. The times are simulated.
32 devices in a mesh: groups: 2 (over y), member: 4 (over x, core), fsdp: 4 (over z).
Axes of the slice: x: 2, y: 2, z: 4, core: 2. Of those that a mesh axis runs over, the one named last changes fastest.
Arguments:
- params: float32 [64, 1024, 1024], P(('groups', 'member'), 'fsdp'), parts along dimension 0, may hold values from -210 to 210
- gradients: bfloat16 [64, 1024, 1024], P(('groups', 'member'), 'fsdp'), parts along dimension 0, may hold values from -1.5258789e-05 to 1.5258789e-05
- first_moment: float32 [64, 1024, 1024], P(('groups', 'member'), 'fsdp'), parts along dimension 0, may hold values from -5.9604645e-07 to 5.9604645e-07
- second_moment: float32 [64, 1024, 1024], P(('groups', 'member'), 'fsdp'), parts along dimension 0, may hold values from 1.8189895e-15 to 3.6379787e-14
Outputs:
- new_params: float32 [64, 1024, 1024], P(('groups', 'member'), 'fsdp'), parts along dimension 0
- new_first: float32 [64, 1024, 1024], P(('groups', 'member'), 'fsdp'), parts along dimension 0
- new_second: float32 [64, 1024, 1024], P(('groups', 'member'), 'fsdp'), parts along dimension 0
- update: float32 [64, 1024, 1024], P(('groups', 'member'), 'fsdp'), parts along dimension 0
- stein_dir: float32 [64, 1024, 1024], P(('groups', 'member'), 'fsdp'), parts along dimension 0
- pair_distance: float32 [64, 32], P('groups'), parts along dimension 0
There are 2 independent parts, one for each index of `groups`. A program takes and returns all parts, laid end to end along the dimension named above; each array names one. Nothing has to cross between parts.
All inputs are finite; a program needn't handle non-finite values.
Results may differ from a plain program's by a relative error of at most 0.0025.
Values may be sent and summed in bfloat16 or wider, within the bound.
No kernel may reach another device: no remote copies, remote signals or barrier semaphores. Data moves between devices by JAX's collectives and lax.ppermute only.
A program may use at most 192 MiB of HBM per device.

v0:
```python
import math
import jax
import jax.numpy as jnp
from jax import lax
from jax.sharding import PartitionSpec as P

STEP_COUNT = 100
decay_first = 0.9
decay_second = 0.95
epsilon = 1e-08
learn_rate = 0.001
weight_decay = 0.05


def kernel_from(gram_total, members):
    self_dots = jnp.diagonal(gram_total)
    sqdist = self_dots[:, None] + self_dots[None, :] - 2.0 * gram_total
    kernel_scale = jnp.sum(sqdist) / (members * (members - 1)) / math.log(members)
    kernel = jnp.exp(-sqdist / kernel_scale)
    return (sqdist, kernel_scale, kernel.astype(jnp.bfloat16))


def adamw_step(params, stein_dir, first_moment, second_moment):
    descent = -stein_dir
    new_first = decay_first * first_moment + (1.0 - decay_first) * descent
    new_second = decay_second * second_moment + (1.0 - decay_second) * descent * descent
    first_hat = new_first / (1.0 - decay_first**STEP_COUNT)
    second_hat = new_second / (1.0 - decay_second**STEP_COUNT)
    update = first_hat / (jnp.sqrt(second_hat) + epsilon) + weight_decay * params
    new_params = params - learn_rate * update
    return (new_params, new_first, new_second, update)


def inner_products(left_flat, right_flat):
    return lax.dot_general(
        left_flat, right_flat, (((1,), (1,)), ((), ())), preferred_element_type=jnp.float32
    )


def shards(params, gradients, first_moment, second_moment):
    members_dev, rows_dev, feature_width = params.shape
    n_member = lax.axis_size("member")
    members = members_dev * n_member
    entries = rows_dev * lax.axis_size("fsdp") * feature_width
    working = params.astype(jnp.bfloat16)
    ascent = -gradients
    wide_work, wide_ascent = (
        lax.all_to_all(working, "member", split_axis=1, concat_axis=0, tiled=True),
        lax.all_to_all(ascent, "member", split_axis=1, concat_axis=0, tiled=True),
    )
    flat_work = wide_work.reshape(members, -1)
    gram_local = inner_products(flat_work, flat_work)
    flat_ascent = wide_ascent.reshape(members, -1)
    gram_total = lax.psum(gram_local, ("member", "fsdp"))
    sqdist, kernel_scale, kernel_half = kernel_from(gram_total, members)
    rowsum = jnp.sum(kernel_half.astype(jnp.float32), axis=1)
    repulse = 2.0 / kernel_scale
    mixed_ascent = jnp.dot(kernel_half, flat_ascent, preferred_element_type=jnp.float32)
    mixed_work = jnp.dot(kernel_half, flat_work, preferred_element_type=jnp.float32)
    stein_mix = (
        mixed_ascent + repulse * (rowsum[:, None] * flat_work.astype(jnp.float32) - mixed_work)
    ) / members
    stein_dir = lax.all_to_all(
        stein_mix.reshape(wide_work.shape), "member", split_axis=0, concat_axis=1, tiled=True
    )
    new_params, new_first, new_second, update = adamw_step(
        params, stein_dir, first_moment, second_moment
    )
    pair_distance = sqdist / entries
    return (new_params, new_first, new_second, update, stein_dir, pair_distance)


def solution(mesh):
    return jax.shard_map(
        shards,
        mesh=mesh,
        in_specs=(
            P(("groups", "member"), "fsdp", None),
            P(("groups", "member"), "fsdp", None),
            P(("groups", "member"), "fsdp", None),
            P(("groups", "member"), "fsdp", None),
        ),
        out_specs=(
            P(("groups", "member"), "fsdp", None),
            P(("groups", "member"), "fsdp", None),
            P(("groups", "member"), "fsdp", None),
            P(("groups", "member"), "fsdp", None),
            P(("groups", "member"), "fsdp", None),
            P("groups", None),
        ),
        check_vma=False,
    )
```

profile of v0, /device:TPU:0, one launch (start us, length us, event | category | flops | bytes accessed | tf_op | source)
XLA Modules:
  0.0 314.9 jit_solution(15781765817421736851)
XLA Ops:
  0.6 6.6 %copy_negate_fusion = bf16[8,256,1024]{2,0,1:T(8,128)(2,1)} fusion(bf16[8,256,1024]{2,1,0:T(8,128)(2,1)} %param.5), kind=kLoop, calls=%fused_computation.12 | loop fusion | flops 2097152 | bytes 8388608 | tf_op jit(solution)/shard_map/neg | solution.py:46
  7.3 4.8 %all-to-all-start.1 = ((bf16[8,256,1024]{2,0,1:T(8,128)(2,1)}), bf16[8,256,1024]{2,0,1:T(8,128)(2,1)}, u32[]{:S(2)}, u32[]{:S(2)}) async-start(bf16[8,256,1024]{2,0,1:T(8,128)(2,1)} %copy_negate_fusion), calls=%async_computation.1 | async-start | bytes 8388608 | tf_op jit(solution)/shard_map/all_to_all | solution.py:49
  12.1 9.8 %copy.24 = bf16[8,256,1024]{2,0,1:T(8,128)(2,1)} copy(f32[8,256,1024]{2,1,0:T(8,128)} %param.4) | data formatting | bytes 12582912 | tf_op args[0]
  22.0 39.0 %all-to-all-done.1 = bf16[8,256,1024]{2,0,1:T(8,128)(2,1)} async-done(((bf16[8,256,1024]{2,0,1:T(8,128)(2,1)}), bf16[8,256,1024]{2,0,1:T(8,128)(2,1)}, u32[]{:S(2)}, u32[]{:S(2)}) %all-to-all-start.1) | async-done | bytes 4194336 | tf_op jit(solution)/shard_map/all_to_all | solution.py:49
  61.0 5.0 %all-to-all-start = ((bf16[8,256,1024]{2,0,1:T(8,128)(2,1)}), bf16[8,256,1024]{2,0,1:T(8,128)(2,1)}, u32[]{:S(2)}, u32[]{:S(2)}) async-start(bf16[8,256,1024]{2,0,1:T(8,128)(2,1)} %copy.24), calls=%async_computation | async-start | bytes 8388608 | tf_op jit(solution)/shard_map/all_to_all | solution.py:48
  66.0 4.5 %copy.25 = bf16[8,4,64,1024]{3,2,0,1:T(8,128)(2,1)S(1)} copy(bf16[8,4,64,1024]{3,0,2,1:T(8,128)(2,1)} %bitcast.4) | data formatting | bytes 8388608 | tf_op jit(solution)/shard_map/all_to_all | solution.py:49
  70.5 4.3 %copy.19 = bf16[4,8,64,1024]{3,1,2,0:T(8,128)(2,1)} copy(bf16[4,8,64,1024]{3,2,1,0:T(8,128)(2,1)S(1)} %bitcast.34) | data formatting | bytes 8388608
  74.9 39.2 %all-to-all-done = bf16[8,256,1024]{2,0,1:T(8,128)(2,1)} async-done(((bf16[8,256,1024]{2,0,1:T(8,128)(2,1)}), bf16[8,256,1024]{2,0,1:T(8,128)(2,1)}, u32[]{:S(2)}, u32[]{:S(2)}) %all-to-all-start) | async-done | bytes 4194336 | tf_op jit(solution)/shard_map/all_to_all | solution.py:48
  114.1 4.7 %fusion.6 = f32[32,32]{1,0:T(8,128)S(1)} fusion(bf16[32,65536]{1,0:T(8,128)(2,1)} %bitcast.2), kind=kOutput, calls=%fused_computation.19 | convolution fusion | flops 134217728 | bytes 4198400 | tf_op jit(solution)/shard_map/dot_general | solution.py:35
  118.7 61.5 %psum.7 = f32[32,32]{1,0:T(8,128)S(1)} all-reduce(f32[32,32]{1,0:T(8,128)S(1)} %fusion.6), channel_id=1, replica_groups=mesh['groups'=2,'member'=4,'fsdp'=4] {'member','fsdp'}, use_global_device_ids=true, to_apply=%region_0.0 | all-reduce | flops 1024 | bytes 8192 | tf_op jit(solution)/shard_map/psum | solution.py:54
  180.2 0.7 gather_fusion
  180.9 1.3 fusion.3
  182.8 0.2 convert_reduce_fusion
  183.1 0.0 copy-start
  183.1 5.1 %fusion = f32[32,65536]{1,0:T(8,128)S(1)} fusion(bf16[32,32]{1,0:T(8,128)(2,1)S(1)} %get-tuple-element.11, bf16[32,65536]{1,0:T(8,128)(2,1)} %bitcast.2, f32[32]{0:T(128)S(1)} %get-tuple-element.10, f32[]{:T(128)S(6)} %div.43), kind=kOutput, calls=%fused_computation.2 | convolution fusion | flops 142606336 | bytes 12585092 | tf_op jit(solution)/shard_map/dot_general | solution.py:59
  188.2 0.0 copy-done
  188.2 1.2 fusion.1
  189.4 4.9 %copy.20 = f32[4,8,64,1024]{3,2,1,0:T(8,128)S(1)} copy(f32[4,8,64,1024]{3,1,2,0:T(8,128)S(1)} %bitcast.27) | data formatting | bytes 16777216
  194.3 0.0 slice-start
  194.3 96.1 %all_to_all.48 = f32[32,64,1024]{2,1,0:T(8,128)S(1)} all-to-all(f32[32,64,1024]{2,1,0:T(8,128)S(1)} %bitcast.28), channel_id=1, replica_groups=mesh['groups'=2,'member'=4,'fsdp'=4] {'member'}, dimensions={0} | all-to-all | bytes 16777216 | tf_op jit(solution)/shard_map/all_to_all | solution.py:63
  290.4 4.3 %copy.18 = f32[4,8,64,1024]{3,2,0,1:T(8,128)} copy(f32[4,8,64,1024]{3,2,1,0:T(8,128)S(1)} %bitcast.29) | data formatting | bytes 16777216 | tf_op jit(solution)/shard_map/all_to_all | solution.py:63
  294.7 0.0 slice-done
  294.7 0.0 slice-done.1
  294.7 20.2 %multiply_subtract_fusion = (f32[8,256,1024]{2,1,0:T(8,128)}, f32[8,256,1024]{2,1,0:T(8,128)}, f32[8,256,1024]{2,1,0:T(8,128)}, f32[8,256,1024]{2,1,0:T(8,128)}) fusion(f32[8,256,1024]{2,1,0:T(8,128)S(1)} %bitcast.31, f32[8,256,1024]{2,1,0:T(8,128)} %param.6, f32[8,256,1024]{2,1,0:T(8,128)} %param.7, f32[4,8,64,1024]{3,2,0,1:T(8,128)} %copy.18), kind=kLoop, calls=%fused_computation.8 | loop fusion | flops 33554432 | bytes 67108864 | tf_op jit(solution)/shard_map/sub | solution.py:30
  (3 shorter events, 0.0 us)
Async XLA Ops:
  7.3 53.7 %all-to-all-start.1 = ((bf16[8,256,1024]{2,0,1:T(8,128)(2,1)}), bf16[8,256,1024]{2,0,1:T(8,128)(2,1)}, u32[]{:S(2)}, u32[]{:S(2)}) async-start(bf16[8,256,1024]{2,0,1:T(8,128)(2,1)} %copy_negate_fusion), calls=%async_computation.1 | async-start | bytes 8388608 | tf_op jit(solution)/shard_map/all_to_all | solution.py:49
  61.0 53.1 %all-to-all-start = ((bf16[8,256,1024]{2,0,1:T(8,128)(2,1)}), bf16[8,256,1024]{2,0,1:T(8,128)(2,1)}, u32[]{:S(2)}, u32[]{:S(2)}) async-start(bf16[8,256,1024]{2,0,1:T(8,128)(2,1)} %copy.24), calls=%async_computation | async-start | bytes 8388608 | tf_op jit(solution)/shard_map/all_to_all | solution.py:48
  183.1 5.1 %copy-start = (bf16[4,8,64,1024]{3,1,2,0:T(8,128)(2,1)S(1)}, bf16[4,8,64,1024]{3,1,2,0:T(8,128)(2,1)}, u32[]{:S(2)}) copy-start(bf16[4,8,64,1024]{3,1,2,0:T(8,128)(2,1)} %copy.19) | copy-start | bytes 12582916
  194.3 100.4 %slice-start = ((s8[8388608]{0:T(1024)(128)(4,1)}), s8[4194304]{0:T(1024)(128)(4,1)S(1)}, s32[]{:S(2)}) async-start(s8[8388608]{0:T(1024)(128)(4,1)} %bitcast.30), calls=%async_computation.3 | async-start | bytes 8388608
  290.4 4.3 %slice-start.1 = ((s8[8388608]{0:T(1024)(128)(4,1)}), s8[4194304]{0:T(1024)(128)(4,1)S(1)}, s32[]{:S(2)}) async-start(s8[8388608]{0:T(1024)(128)(4,1)} %bitcast.30), calls=%async_computation.4 | async-start | bytes 8388608
where the time goes:
time: 315 us
  blocking collectives  158 us (50%)
  waiting for transfers between devices  78.2 us (25%)
  local copies, waits for them, and re-layouts  28.6 us (9%)
  other arithmetic  28.3 us (9%)
  matrix products  11 us (3%)
  starting transfers between devices  9.86 us (3%)
    all_to_all x1, blocking collectives, shards(): lax.all_to_all(stein_mix.reshape(wide_work.shape), 'member', split_axis=0...  96.1 us
    psum x1, blocking collectives, shards(): gram_total = lax.psum(gram_local, ('member', 'fsdp'))  61.5 us
    all_to_all x1, waiting for transfers between devices, shards(): lax.all_to_all(working, 'member', split_axis=1, concat_axis=0, tiled=True)  39.2 us
    all_to_all x1, waiting for transfers between devices, shards(): lax.all_to_all(ascent, 'member', split_axis=1, concat_axis=0, tiled=True)  39 us
    sub x1, other arithmetic, adamw_step(): new_params = params - learn_rate * update  20.2 us
    unnamed x9, local copies, waits for them, and re-layouts  19.1 us
    neg x1, other arithmetic, shards(): ascent = -gradients  6.63 us
  transfers between devices with their start and end apart: 2, of which 2 were waited for; matrix products, arithmetic and copies ran while one was open for 6% of the time, Pallas kernels for 0%

commit v1 on v0

--- a/solution.py
+++ b/solution.py
@@ -51,7 +51,7 @@
     flat_work = wide_work.reshape(members, -1)
     gram_local = inner_products(flat_work, flat_work)
     flat_ascent = wide_ascent.reshape(members, -1)
-    gram_total = lax.psum(gram_local, ("member", "fsdp"))
+    gram_total = lax.psum(lax.psum(gram_local, "fsdp"), "member")
     sqdist, kernel_scale, kernel_half = kernel_from(gram_total, members)
     rowsum = jnp.sum(kernel_half.astype(jnp.float32), axis=1)
     repulse = 2.0 / kernel_scale

time: 315 us -> 284 us (0.902)
  blocking collectives: 158 us -> 126 us
    psum x1 -> x2, blocking collectives: 61.5 us -> 30.1 us  [shards(): gram_total = lax.psum(lax.psum(gram_local, 'fsdp'), 'member')]
  transfers between devices with their start and end apart: 2 -> 2, of which waited for: 2 -> 2; matrix products, arithmetic and copies ran while one was open for 6% -> 7% of each run, Pallas kernels for 0% -> 0%
where the time goes in v1:
time: 284 us
  blocking collectives  126 us (44%)
  waiting for transfers between devices  78.2 us (28%)
  local copies, waits for them, and re-layouts  28.6 us (10%)
  other arithmetic  28.3 us (10%)
  matrix products  11 us (4%)
  starting transfers between devices  9.88 us (3%)
    all_to_all x1, blocking collectives, shards(): lax.all_to_all(stein_mix.reshape(wide_work.shape), 'member', split_axis=0...  96.1 us
    all_to_all x1, waiting for transfers between devices, shards(): lax.all_to_all(working, 'member', split_axis=1, concat_axis=0, tiled=True)  39.2 us
    all_to_all x1, waiting for transfers between devices, shards(): lax.all_to_all(ascent, 'member', split_axis=1, concat_axis=0, tiled=True)  39 us
    psum x2, blocking collectives, shards(): gram_total = lax.psum(lax.psum(gram_local, 'fsdp'), 'member')  30.1 us
    sub x1, other arithmetic, adamw_step(): new_params = params - learn_rate * update  20.2 us
    unnamed x9, local copies, waits for them, and re-layouts  19.1 us
    neg x1, other arithmetic, shards(): ascent = -gradients  6.63 us
  transfers between devices with their start and end apart: 2, of which 2 were waited for; matrix products, arithmetic and copies ran while one was open for 7% of the time, Pallas kernels for 0%

profile of v1, /device:TPU:0, one launch (start us, length us, event | category | flops | bytes accessed | tf_op | source)
XLA Modules:
  0.0 283.6 jit_solution(7114200165911964696)
XLA Ops:
  0.6 6.6 %copy_negate_fusion = bf16[8,256,1024]{2,0,1:T(8,128)(2,1)} fusion(bf16[8,256,1024]{2,1,0:T(8,128)(2,1)} %param.5), kind=kLoop, calls=%fused_computation.12 | loop fusion | flops 2097152 | bytes 8388608 | tf_op jit(solution)/shard_map/neg | solution.py:46
  7.3 4.8 %all-to-all-start.1 = ((bf16[8,256,1024]{2,0,1:T(8,128)(2,1)}), bf16[8,256,1024]{2,0,1:T(8,128)(2,1)}, u32[]{:S(2)}, u32[]{:S(2)}) async-start(bf16[8,256,1024]{2,0,1:T(8,128)(2,1)} %copy_negate_fusion), calls=%async_computation.1 | async-start | bytes 8388608 | tf_op jit(solution)/shard_map/all_to_all | solution.py:49
  12.1 9.8 %copy.24 = bf16[8,256,1024]{2,0,1:T(8,128)(2,1)} copy(f32[8,256,1024]{2,1,0:T(8,128)} %param.4) | data formatting | bytes 12582912 | tf_op args[0]
  22.0 39.0 %all-to-all-done.1 = bf16[8,256,1024]{2,0,1:T(8,128)(2,1)} async-done(((bf16[8,256,1024]{2,0,1:T(8,128)(2,1)}), bf16[8,256,1024]{2,0,1:T(8,128)(2,1)}, u32[]{:S(2)}, u32[]{:S(2)}) %all-to-all-start.1) | async-done | bytes 4194336 | tf_op jit(solution)/shard_map/all_to_all | solution.py:49
  61.0 5.0 %all-to-all-start = ((bf16[8,256,1024]{2,0,1:T(8,128)(2,1)}), bf16[8,256,1024]{2,0,1:T(8,128)(2,1)}, u32[]{:S(2)}, u32[]{:S(2)}) async-start(bf16[8,256,1024]{2,0,1:T(8,128)(2,1)} %copy.24), calls=%async_computation | async-start | bytes 8388608 | tf_op jit(solution)/shard_map/all_to_all | solution.py:48
  66.0 4.5 %copy.25 = bf16[8,4,64,1024]{3,2,0,1:T(8,128)(2,1)S(1)} copy(bf16[8,4,64,1024]{3,0,2,1:T(8,128)(2,1)} %bitcast.4) | data formatting | bytes 8388608 | tf_op jit(solution)/shard_map/all_to_all | solution.py:49
  70.5 4.3 %copy.19 = bf16[4,8,64,1024]{3,1,2,0:T(8,128)(2,1)} copy(bf16[4,8,64,1024]{3,2,1,0:T(8,128)(2,1)S(1)} %bitcast.34) | data formatting | bytes 8388608
  74.9 39.2 %all-to-all-done = bf16[8,256,1024]{2,0,1:T(8,128)(2,1)} async-done(((bf16[8,256,1024]{2,0,1:T(8,128)(2,1)}), bf16[8,256,1024]{2,0,1:T(8,128)(2,1)}, u32[]{:S(2)}, u32[]{:S(2)}) %all-to-all-start) | async-done | bytes 4194336 | tf_op jit(solution)/shard_map/all_to_all | solution.py:48
  114.1 4.7 %fusion.6 = f32[32,32]{1,0:T(8,128)S(1)} fusion(bf16[32,65536]{1,0:T(8,128)(2,1)} %bitcast.2), kind=kOutput, calls=%fused_computation.19 | convolution fusion | flops 134217728 | bytes 4198400 | tf_op jit(solution)/shard_map/dot_general | solution.py:35
  118.7 19.8 %psum.14 = f32[32,32]{1,0:T(8,128)S(1)} all-reduce(f32[32,32]{1,0:T(8,128)S(1)} %fusion.6), channel_id=1, replica_groups=mesh['groups'=2,'member'=4,'fsdp'=4] {'fsdp'}, use_global_device_ids=true, to_apply=%region_0.0 | all-reduce | flops 1024 | bytes 8192 | tf_op jit(solution)/shard_map/psum | solution.py:54
  138.6 10.3 %psum.15 = f32[32,32]{1,0:T(8,128)S(1)} all-reduce(f32[32,32]{1,0:T(8,128)S(1)} %psum.14), channel_id=1, replica_groups=mesh['groups'=2,'member'=4,'fsdp'=4] {'member'}, use_global_device_ids=true, to_apply=%region_1.0 | all-reduce | flops 1024 | bytes 8192 | tf_op jit(solution)/shard_map/psum | solution.py:54
  148.9 0.7 gather_fusion
  149.6 1.3 fusion.3
  151.5 0.2 convert_reduce_fusion
  151.8 0.0 copy-start
  151.8 5.1 %fusion = f32[32,65536]{1,0:T(8,128)S(1)} fusion(bf16[32,32]{1,0:T(8,128)(2,1)S(1)} %get-tuple-element.11, bf16[32,65536]{1,0:T(8,128)(2,1)} %bitcast.2, f32[32]{0:T(128)S(1)} %get-tuple-element.10, f32[]{:T(128)S(6)} %div.43), kind=kOutput, calls=%fused_computation.2 | convolution fusion | flops 142606336 | bytes 12585092 | tf_op jit(solution)/shard_map/dot_general | solution.py:59
  156.9 0.0 copy-done
  156.9 1.2 fusion.1
  158.1 4.9 %copy.20 = f32[4,8,64,1024]{3,2,1,0:T(8,128)S(1)} copy(f32[4,8,64,1024]{3,1,2,0:T(8,128)S(1)} %bitcast.27) | data formatting | bytes 16777216
  163.0 0.0 slice-start
  163.0 96.1 %all_to_all.48 = f32[32,64,1024]{2,1,0:T(8,128)S(1)} all-to-all(f32[32,64,1024]{2,1,0:T(8,128)S(1)} %bitcast.28), channel_id=1, replica_groups=mesh['groups'=2,'member'=4,'fsdp'=4] {'member'}, dimensions={0} | all-to-all | bytes 16777216 | tf_op jit(solution)/shard_map/all_to_all | solution.py:63
  259.1 4.3 %copy.18 = f32[4,8,64,1024]{3,2,0,1:T(8,128)} copy(f32[4,8,64,1024]{3,2,1,0:T(8,128)S(1)} %bitcast.29) | data formatting | bytes 16777216 | tf_op jit(solution)/shard_map/all_to_all | solution.py:63
  263.4 0.0 slice-done
  263.4 20.2 %multiply_subtract_fusion = (f32[8,256,1024]{2,1,0:T(8,128)}, f32[8,256,1024]{2,1,0:T(8,128)}, f32[8,256,1024]{2,1,0:T(8,128)}, f32[8,256,1024]{2,1,0:T(8,128)}) fusion(f32[8,256,1024]{2,1,0:T(8,128)S(1)} %bitcast.31, f32[8,256,1024]{2,1,0:T(8,128)} %param.6, f32[8,256,1024]{2,1,0:T(8,128)} %param.7, f32[4,8,64,1024]{3,2,0,1:T(8,128)} %copy.18), kind=kLoop, calls=%fused_computation.8 | loop fusion | flops 33554432 | bytes 67108864 | tf_op jit(solution)/shard_map/sub | solution.py:30
  (4 shorter events, 0.0 us)
Async XLA Ops:
  7.3 53.7 %all-to-all-start.1 = ((bf16[8,256,1024]{2,0,1:T(8,128)(2,1)}), bf16[8,256,1024]{2,0,1:T(8,128)(2,1)}, u32[]{:S(2)}, u32[]{:S(2)}) async-start(bf16[8,256,1024]{2,0,1:T(8,128)(2,1)} %copy_negate_fusion), calls=%async_computation.1 | async-start | bytes 8388608 | tf_op jit(solution)/shard_map/all_to_all | solution.py:49
  61.0 53.1 %all-to-all-start = ((bf16[8,256,1024]{2,0,1:T(8,128)(2,1)}), bf16[8,256,1024]{2,0,1:T(8,128)(2,1)}, u32[]{:S(2)}, u32[]{:S(2)}) async-start(bf16[8,256,1024]{2,0,1:T(8,128)(2,1)} %copy.24), calls=%async_computation | async-start | bytes 8388608 | tf_op jit(solution)/shard_map/all_to_all | solution.py:48
  151.8 5.1 %copy-start = (bf16[4,8,64,1024]{3,1,2,0:T(8,128)(2,1)S(1)}, bf16[4,8,64,1024]{3,1,2,0:T(8,128)(2,1)}, u32[]{:S(2)}) copy-start(bf16[4,8,64,1024]{3,1,2,0:T(8,128)(2,1)} %copy.19) | copy-start | bytes 12582916
  163.0 100.4 %slice-start = ((s8[8388608]{0:T(1024)(128)(4,1)}), s8[4194304]{0:T(1024)(128)(4,1)S(1)}, s32[]{:S(2)}) async-start(s8[8388608]{0:T(1024)(128)(4,1)} %bitcast.30), calls=%async_computation.3 | async-start | bytes 8388608
  259.1 4.3 %slice-start.1 = ((s8[8388608]{0:T(1024)(128)(4,1)}), s8[4194304]{0:T(1024)(128)(4,1)S(1)}, s32[]{:S(2)}) async-start(s8[8388608]{0:T(1024)(128)(4,1)} %bitcast.30), calls=%async_computation.4 | async-start | bytes 8388608
